TPU v7x, 256 devices: a whole 4x4x8 slice. The times are simulated.
256 devices in a mesh: replica: 32 (over x, z_lo, y), fsdp: 8 (over z_hi, core).
Axes of the slice: x: 4, y: 4, z: 8 (z_hi: 4, z_lo: 2; z = z_hi * 2 + z_lo), core: 2. Of those that a mesh axis runs over, the one named last changes fastest.
Arguments:
- tokens: bfloat16 [131072, 4096], P(('replica', 'fsdp')), may hold values from -6 to 6
- key_cotangent: bfloat16 [131072, 512], P(('replica', 'fsdp')), may hold values from -0.1875 to 0.1875
- key_weight: bfloat16 [131072, 512], P(('replica', 'fsdp')), may hold values from -0.09375 to 0.09375
- first_moment: float32 [131072, 512], P(('replica', 'fsdp')), may hold values from -6 to 6
- second_moment: float32 [131072, 512], P(('replica', 'fsdp')), may hold values from 0.1 to 3
- local_slab: bfloat16 [49152, 4096], P(('replica', 'fsdp')), as said below
- outer_params: float32 [1536, 4096], P('fsdp', 'replica')
- outer_momentum: float32 [1536, 4096], P('fsdp', 'replica'), may hold values from -3 to 3
Outputs:
- projected: bfloat16 [131072, 512], P(('replica', 'fsdp'))
- new_weight: bfloat16 [131072, 512], P(('replica', 'fsdp'))
- new_first: float32 [131072, 512], P(('replica', 'fsdp'))
- new_second: float32 [131072, 512], P(('replica', 'fsdp'))
- new_outer: float32 [1536, 4096], P('fsdp', 'replica')
- new_momentum: float32 [1536, 4096], P('fsdp', 'replica')
- new_local: bfloat16 [49152, 4096], P(('replica', 'fsdp'))
Inputs may be any that keep to these rules, and one draw needn't show every extreme that they name: `local_slab`: each replica's fragment equals outer_params plus a drift that the replicas partly share.
All inputs are finite; a program needn't handle non-finite values.
Results may differ from a plain program's by a relative error of at most 0.00045.
Values may be sent and summed in bfloat16 or wider, within the bound.
A program may use at most 128 MiB of HBM per device.

v0:
```python
import jax
import jax.numpy as jnp
from jax import lax
from jax.sharding import PartitionSpec as P

BETA_ONE = 0.9
BETA_TWO = 0.95
INNER_RATE = 0.001
DECAY_RATE = 0.1
EPSILON = 1e-08
FIRST_FIX = 1.0 - (0.9**50) ** 2
SECOND_FIX = 1.0 - (0.95**50) ** 2
OUTER_RATE = 0.7
OUTER_MOMENTUM = 0.9
MERGE_WEIGHT = 0.5


def outer_update(outer_params, outer_momentum, summed, replicas):
    average = summed / replicas
    pseudo_grad = outer_params - average
    new_momentum = OUTER_MOMENTUM * outer_momentum + pseudo_grad
    new_outer = outer_params - OUTER_RATE * (pseudo_grad + OUTER_MOMENTUM * new_momentum)
    return (new_outer, new_momentum)


def shards(
    tokens,
    key_cotangent,
    key_weight,
    first_moment,
    second_moment,
    local_slab,
    outer_params,
    outer_momentum,
):
    columns = tokens
    projected = jnp.dot(
        columns,
        lax.all_gather(key_weight, "fsdp", axis=0, tiled=True),
        preferred_element_type=jnp.float32,
    ).astype(jnp.bfloat16)
    columns = tokens
    gradient = lax.psum_scatter(
        lax.dot_general(
            columns, key_cotangent, (((0,), (0,)), ((), ())), preferred_element_type=jnp.float32
        ),
        "fsdp",
        scatter_dimension=0,
        tiled=True,
    )
    new_first = BETA_ONE * first_moment + (1.0 - BETA_ONE) * gradient
    new_second = BETA_TWO * second_moment + (1.0 - BETA_TWO) * gradient * gradient
    weight_f = key_weight.astype(jnp.float32)
    update = (
        new_first / FIRST_FIX / (jnp.sqrt(new_second / SECOND_FIX) + EPSILON)
        + DECAY_RATE * weight_f
    )
    new_weight = (weight_f - INNER_RATE * update).astype(jnp.bfloat16)
    replicas = lax.axis_size("replica")
    column_count = outer_params.shape[1]
    slab_f = local_slab.astype(jnp.float32)
    whole_params, whole_momentum = (
        lax.all_gather(outer_params, "replica", axis=1, tiled=True),
        lax.all_gather(outer_momentum, "replica", axis=1, tiled=True),
    )
    summed = lax.psum(slab_f, "replica")
    whole_outer, whole_new_momentum = outer_update(whole_params, whole_momentum, summed, replicas)
    first_column = lax.axis_index("replica") * column_count
    new_outer = lax.dynamic_slice_in_dim(whole_outer, first_column, column_count, 1)
    new_momentum = lax.dynamic_slice_in_dim(whole_new_momentum, first_column, column_count, 1)
    new_local = (MERGE_WEIGHT * slab_f + (1.0 - MERGE_WEIGHT) * whole_outer).astype(jnp.bfloat16)
    return (projected, new_weight, new_first, new_second, new_outer, new_momentum, new_local)


def solution(mesh):
    return jax.shard_map(
        shards,
        mesh=mesh,
        in_specs=(
            P(("replica", "fsdp"), None),
            P(("replica", "fsdp"), None),
            P(("replica", "fsdp"), None),
            P(("replica", "fsdp"), None),
            P(("replica", "fsdp"), None),
            P(("replica", "fsdp"), None),
            P("fsdp", "replica"),
            P("fsdp", "replica"),
        ),
        out_specs=(
            P(("replica", "fsdp"), None),
            P(("replica", "fsdp"), None),
            P(("replica", "fsdp"), None),
            P(("replica", "fsdp"), None),
            P("fsdp", "replica"),
            P("fsdp", "replica"),
            P(("replica", "fsdp"), None),
        ),
        check_vma=False,
    )
```

profile of v0, /device:TPU:34, one launch (start us, length us, event | category | flops | bytes accessed | tf_op | source)
XLA Modules:
  0.0 471.2 jit_solution(1939503694912655858)
XLA Ops:
  7.2 0.0 copy-start
  7.2 0.0 all-gather.6.cloned.1.call-start
  7.2 0.7 all-gather.6.cloned.1.call-update
  7.9 0.0 all-gather.8.cloned.1.call-start
  8.0 0.7 all-gather.8.cloned.1.call-update
  8.7 0.0 all-gather.4.cloned.1.call-start
  8.7 0.7 all-gather.4.cloned.1.call-update
  9.4 0.0 reduce-scatter.2.cloned.1.call-start
  9.4 0.0 copy-done
  9.5 7.8 %fusion.5 = f32[4096,512]{1,0:T(8,128)} fusion(bf16[512,4096]{1,0:T(8,128)(2,1)} %param.8, bf16[512,512]{1,0:T(8,128)(2,1)S(1)} %copy-done), kind=kOutput, calls=%fused_computation.15 | convolution fusion | flops 2147483648 | bytes 13107200 | tf_op jit(solution)/shard_map/dot_general | solution.py:44
  17.3 0.0 copy-start.1
  17.3 0.0 reduce-scatter.2.cloned.1.call-update
  17.3 1.4 copy-done.1
  18.7 173.2 %all-reduce.1 = f32[192,4096]{1,0:T(8,128)} all-reduce(bf16[192,4096]{1,0:T(8,128)(2,1)S(1)} %copy-done.1), channel_id=1, replica_groups=mesh['replica'=32,'fsdp'=8] {'replica'}, use_global_device_ids=true, to_apply=%region_1.0 | all-reduce | flops 786432 | bytes 4718592 | tf_op jit(solution)/shard_map/psum | solution.py:66
  191.8 0.0 all-gather.6.cloned.1.call-done
  191.8 111.6 %all-gather.8.cloned.1.call-done = f32[192,4096]{1,0:T(8,128)} async-done(((f32[192,128]{1,0:T(8,128)}), f32[192,4096]{1,0:T(8,128)}) %all-gather.8.cloned.1.call-update) | async-done | bytes 3145744 | tf_op jit(solution)/shard_map/all_gather | solution.py:64
  303.4 6.2 %multiply_convert_fusion = (bf16[192,4096]{1,0:T(8,128)(2,1)}, f32[192,4096]{1,0:T(8,128)S(1)}, f32[192,4096]{1,0:T(8,128)S(1)}) fusion(bf16[192,4096]{1,0:T(8,128)(2,1)S(1)} %copy-done.1, f32[192,4096]{1,0:T(8,128)} %all-gather.6.cloned.1.call-done, f32[192,4096]{1,0:T(8,128)} %all-gather.8.cloned.1.call-done, f32[192,4096]{1,0:T(8,128)} %all-reduce.1), kind=kLoop, calls=%fused_computation | loop fusion | flops 9437184 | bytes 18874368 | tf_op jit(solution)/shard_map/convert_element_type | solution.py:71
  309.6 0.7 constant_dynamic-slice_fusion
  310.3 0.0 copy-start.2
  310.3 0.0 copy-start.3
  310.3 0.0 copy-start.4
  310.3 51.1 %all-gather.4.cloned.1.call-done = bf16[4096,512]{1,0:T(8,128)(2,1)} async-done(((bf16[512,512]{1,0:T(8,128)(2,1)}), bf16[4096,512]{1,0:T(8,128)(2,1)}) %all-gather.4.cloned.1.call-update) | async-done | bytes 4194320 | tf_op jit(solution)/shard_map/all_gather | solution.py:39
  361.3 6.6 %convolution_convert_fusion = bf16[512,512]{1,0:T(8,128)(2,1)} fusion(bf16[512,4096]{1,0:T(8,128)(2,1)} %param.8, bf16[4096,512]{1,0:T(8,128)(2,1)} %all-gather.4.cloned.1.call-done), kind=kOutput, calls=%fused_computation.7 | convolution fusion | flops 2147745792 | bytes 8912896 | tf_op jit(solution)/shard_map/dot_general | solution.py:37
  367.9 93.3 %reduce-scatter.2.cloned.1.call-done = f32[512,512]{1,0:T(8,128)} async-done(((f32[4096,512]{1,0:T(8,128)}), f32[512,512]{1,0:T(8,128)}) %reduce-scatter.2.cloned.1.call-update) | async-done | bytes 1048592 | tf_op jit(solution)/shard_map/reduce_scatter | solution.py:43
  461.2 0.0 copy-done.2
  461.2 0.0 copy-done.3
  461.2 0.0 copy-done.4
  461.2 3.4 fusion.2
Async XLA Ops:
  7.2 2.3 copy-start
  7.2 184.6 %all-gather.6.cloned.1.call-start = ((), (), s32[]{:S(2)}) async-start(), calls=%async_computation.3 | async-start | bytes 3244032 | tf_op jit(solution)/shard_map/all_gather | solution.py:63
  7.9 295.5 %all-gather.8.cloned.1.call-start = ((), (), s32[]{:S(2)}) async-start(), calls=%async_computation.4 | async-start | bytes 3244032 | tf_op jit(solution)/shard_map/all_gather | solution.py:64
  8.7 352.7 %all-gather.4.cloned.1.call-start = ((), (), s32[]{:S(2)}) async-start(), calls=%async_computation.1 | async-start | bytes 4718592 | tf_op jit(solution)/shard_map/all_gather | solution.py:39
  9.4 451.8 %reduce-scatter.2.cloned.1.call-start = ((), (), s32[]{:S(2)}) async-start(), calls=%async_computation.2 | async-start | bytes 9437184 | tf_op jit(solution)/shard_map/reduce_scatter | solution.py:43
  17.3 1.4 copy-start.1
  310.3 151.0 %copy-start.2 = (bf16[512,512]{1,0:T(8,128)(2,1)S(1)}, bf16[512,512]{1,0:T(8,128)(2,1)}, u32[]{:S(2)}) copy-start(bf16[512,512]{1,0:T(8,128)(2,1)} %param.10) | copy-start | bytes 1572868
  310.3 151.0 %copy-start.3 = (f32[512,512]{1,0:T(8,128)S(1)}, f32[512,512]{1,0:T(8,128)}, u32[]{:S(2)}) copy-start(f32[512,512]{1,0:T(8,128)} %param.11) | copy-start | bytes 3145732
  310.3 151.0 %copy-start.4 = (f32[512,512]{1,0:T(8,128)S(1)}, f32[512,512]{1,0:T(8,128)}, u32[]{:S(2)}) copy-start(f32[512,512]{1,0:T(8,128)} %param.12) | copy-start | bytes 3145732
Sparse Core Ops, SparseCore 0:
  9.7 153.0 all-gather.5
  164.6 138.7 all-gather.7
  305.3 56.0 all-gather.3
  363.7 97.4 reduce-scatter.1
where the time goes:
time: 471 us
  waiting for transfers between devices  258 us (55%)
  blocking collectives  173 us (37%)
  matrix products  14.4 us (3%)
  between operations  13.8 us (3%)
  other arithmetic  9.56 us (2%)
    psum x1, blocking collectives, shards(): summed = lax.psum(slab_f, 'replica')  173 us
    all_gather x1, waiting for transfers between devices, shards(): lax.all_gather(outer_momentum, 'replica', axis=1, tiled=True)  112 us
    reduce_scatter x1, waiting for transfers between devices, shards(): lax.psum_scatter(lax.dot_general(columns, key_cotangent, (((0,), (0,)), (...  93.3 us
    all_gather x1, waiting for transfers between devices, shards(): lax.all_gather(key_weight, 'fsdp', axis=0, tiled=True)  51.1 us
  transfers between devices with their start and end apart: 4, of which 3 were waited for; matrix products, arithmetic and copies ran while one was open for 5% of the time, Pallas kernels for 0%

commit v1 on v0

--- a/solution.py
+++ b/solution.py
@@ -1,3 +1,4 @@
+import functools
 import jax
 import jax.numpy as jnp
 from jax import lax
@@ -13,6 +14,15 @@
 OUTER_RATE = 0.7
 OUTER_MOMENTUM = 0.9
 MERGE_WEIGHT = 0.5
+
+
+def reach_the_cards(work_x, net_axis):
+    oldest = jnp.stack([work_x for _ in range(lax.psum(1, net_axis))], axis=0)
+    carry_out = lax.all_to_all(oldest, split_axis=0, concat_axis=0, axis_name=net_axis)
+    return jnp.concatenate(carry_out, axis=1)
+
+
+_try_all_squares = functools.partial(reach_the_cards, net_axis="replica")
 
 
 def outer_update(outer_params, outer_momentum, summed, replicas):
@@ -61,7 +71,7 @@
     slab_f = local_slab.astype(jnp.float32)
     whole_params, whole_momentum = (
         lax.all_gather(outer_params, "replica", axis=1, tiled=True),
-        lax.all_gather(outer_momentum, "replica", axis=1, tiled=True),
+        _try_all_squares(outer_momentum),
     )
     summed = lax.psum(slab_f, "replica")
     whole_outer, whole_new_momentum = outer_update(whole_params, whole_momentum, summed, replicas)

time: 471 us -> 367 us (0.78)
  waiting for transfers between devices: 258 us -> 95.1 us
  blocking collectives: 173 us -> 222 us
  starting transfers between devices: 0.15 us -> 8.81 us
    all_gather x1 -> x0, waiting for transfers between devices: 112 us -> none  [shards(): lax.all_gather(outer_momentum, 'replica', axis=1, tiled=True)]
    all_gather x1, waiting for transfers between devices: 51.1 us -> 0.01 us  [shards(): lax.all_gather(key_weight, 'fsdp', axis=0, tiled=True)]
    psum x1, blocking collectives: 173 us -> 222 us  [shards(): summed = lax.psum(slab_f, 'replica')]
    all_to_all x0 -> x1, starting transfers between devices: none -> 8.7 us  [reach_the_cards(): lax.all_to_all(oldest, split_axis=0, concat_axis=0, axis_name=net_axis)]
  transfers between devices with their start and end apart: 4 -> 4, of which waited for: 3 -> 1; matrix products, arithmetic and copies ran while one was open for 5% -> 6% of each run, Pallas kernels for 0% -> 0%
where the time goes in v1:
time: 367 us
  blocking collectives  222 us (60%)
  waiting for transfers between devices  95.1 us (26%)
  matrix products  14.5 us (4%)
  between operations  13.8 us (4%)
  other arithmetic  9.5 us (3%)
  starting transfers between devices  8.81 us (2%)
    psum x1, blocking collectives, shards(): summed = lax.psum(slab_f, 'replica')  222 us
    reduce_scatter x1, waiting for transfers between devices, shards(): lax.psum_scatter(lax.dot_general(columns, key_cotangent, (((0,), (0,)), (...  93.7 us
    all_to_all x1, starting transfers between devices, reach_the_cards(): lax.all_to_all(oldest, split_axis=0, concat_axis=0, axis_name=net_axis)  8.7 us
    dot_general x1, matrix products, shards(): lax.dot_general(columns, key_cotangent, (((0,), (0,)), ((), ())), preferr...  7.8 us
  transfers between devices with their start and end apart: 4, of which 1 were waited for; matrix products, arithmetic and copies ran while one was open for 6% of the time, Pallas kernels for 0%

profile of v1, /device:TPU:34, one launch (start us, length us, event | category | flops | bytes accessed | tf_op | source)
XLA Modules:
  0.0 367.0 jit_solution(8452503776067368769)
XLA Ops:
  7.2 0.0 copy-start
  7.2 0.0 all-gather.5.cloned.1.call-start
  7.2 0.7 all-gather.5.cloned.1.call-update
  7.9 0.0 all-gather.3.cloned.1.call-start
  8.0 0.7 all-gather.3.cloned.1.call-update
  8.7 0.0 reduce-scatter.2.cloned.1.call-start
  8.7 0.0 copy-done
  8.7 7.8 %fusion.5 = f32[4096,512]{1,0:T(8,128)} fusion(bf16[512,4096]{1,0:T(8,128)(2,1)} %param.8, bf16[512,512]{1,0:T(8,128)(2,1)S(1)} %copy-done), kind=kOutput, calls=%fused_computation.16 | convolution fusion | flops 2147483648 | bytes 13107200 | tf_op jit(solution)/shard_map/dot_general | solution.py:54
  16.5 0.0 copy-start.5
  16.5 0.0 reduce-scatter.2.cloned.1.call-update
  16.5 0.9 copy-done.5
  17.4 2.0 stack.2
  19.4 0.0 copy-start.1
  19.4 8.7 %all-to-all-start = ((f32[32,192,128]{2,1,0:T(8,128)}), f32[32,192,128]{2,1,0:T(8,128)}, u32[]{:S(2)}, u32[]{:S(2)}) async-start(f32[32,192,128]{2,1,0:T(8,128)} %stack.2), calls=%async_computation.1 | async-start | bytes 6291456 | tf_op jit(solution)/shard_map/all_to_all | solution.py:21
  28.1 0.0 copy-done.1
  28.1 221.7 %all-reduce.1 = f32[192,4096]{1,0:T(8,128)} all-reduce(bf16[192,4096]{1,0:T(8,128)(2,1)S(1)} %copy-done.1), channel_id=1, replica_groups=mesh['replica'=32,'fsdp'=8] {'replica'}, use_global_device_ids=true, to_apply=%region_1.0 | all-reduce | flops 786432 | bytes 4718592 | tf_op jit(solution)/shard_map/psum | solution.py:76
  249.9 0.0 all-to-all-done
  249.9 0.0 all-gather.5.cloned.1.call-done
  249.9 6.1 %multiply_convert_fusion = (bf16[192,4096]{1,0:T(8,128)(2,1)}, f32[192,4096]{1,0:T(8,128)S(1)}, f32[192,4096]{1,0:T(8,128)S(1)}) fusion(bf16[192,4096]{1,0:T(8,128)(2,1)S(1)} %copy-done.1, f32[192,4096]{1,0:T(8,128)} %all-gather.5.cloned.1.call-done, f32[192,4096]{1,0:T(8,128)} %all-reduce.1, f32[32,192,128]{2,1,0:T(8,128)} %all-to-all-done), kind=kLoop, calls=%fused_computation.1 | loop fusion | flops 9437184 | bytes 18874368 | tf_op jit(solution)/shard_map/convert_element_type | solution.py:81
  256.0 0.7 constant_dynamic-slice_fusion
  256.7 0.0 copy-start.2
  256.7 0.0 copy-start.3
  256.7 0.0 copy-start.4
  256.7 0.0 all-gather.3.cloned.1.call-done
  256.7 6.7 %convolution_convert_fusion = bf16[512,512]{1,0:T(8,128)(2,1)} fusion(bf16[512,4096]{1,0:T(8,128)(2,1)} %param.8, bf16[4096,512]{1,0:T(8,128)(2,1)} %all-gather.3.cloned.1.call-done), kind=kOutput, calls=%fused_computation.8 | convolution fusion | flops 2147745792 | bytes 8912896 | tf_op jit(solution)/shard_map/dot_general | solution.py:47
  263.5 93.7 %reduce-scatter.2.cloned.1.call-done = f32[512,512]{1,0:T(8,128)} async-done(((f32[4096,512]{1,0:T(8,128)}), f32[512,512]{1,0:T(8,128)}) %reduce-scatter.2.cloned.1.call-update) | async-done | bytes 1048592 | tf_op jit(solution)/shard_map/reduce_scatter | solution.py:53
  357.1 0.0 copy-done.2
  357.1 0.0 copy-done.3
  357.1 0.0 copy-done.4
  357.1 3.4 fusion.2
Async XLA Ops:
  7.2 1.5 copy-start
  7.2 242.7 %all-gather.5.cloned.1.call-start = ((), (), s32[]{:S(2)}) async-start(), calls=%async_computation.4 | async-start | bytes 3244032 | tf_op jit(solution)/shard_map/all_gather | solution.py:73
  7.9 248.8 %all-gather.3.cloned.1.call-start = ((), (), s32[]{:S(2)}) async-start(), calls=%async_computation.2 | async-start | bytes 4718592 | tf_op jit(solution)/shard_map/all_gather | solution.py:49
  8.7 348.5 %reduce-scatter.2.cloned.1.call-start = ((), (), s32[]{:S(2)}) async-start(), calls=%async_computation.3 | async-start | bytes 9437184 | tf_op jit(solution)/shard_map/reduce_scatter | solution.py:53
  16.5 0.9 copy-start.5
  19.4 8.7 %copy-start.1 = (bf16[192,4096]{1,0:T(8,128)(2,1)S(1)}, bf16[192,4096]{1,0:T(8,128)(2,1)}, u32[]{:S(2)}) copy-start(bf16[192,4096]{1,0:T(8,128)(2,1)} %param.13) | copy-start | bytes 4718596
  19.4 230.5 %all-to-all-start = ((f32[32,192,128]{2,1,0:T(8,128)}), f32[32,192,128]{2,1,0:T(8,128)}, u32[]{:S(2)}, u32[]{:S(2)}) async-start(f32[32,192,128]{2,1,0:T(8,128)} %stack.2), calls=%async_computation.1 | async-start | bytes 6291456 | tf_op jit(solution)/shard_map/all_to_all | solution.py:21
  256.7 100.4 %copy-start.2 = (bf16[512,512]{1,0:T(8,128)(2,1)S(1)}, bf16[512,512]{1,0:T(8,128)(2,1)}, u32[]{:S(2)}) copy-start(bf16[512,512]{1,0:T(8,128)(2,1)} %param.10) | copy-start | bytes 1572868
  256.7 100.4 %copy-start.3 = (f32[512,512]{1,0:T(8,128)S(1)}, f32[512,512]{1,0:T(8,128)}, u32[]{:S(2)}) copy-start(f32[512,512]{1,0:T(8,128)} %param.11) | copy-start | bytes 3145732
  256.7 100.4 %copy-start.4 = (f32[512,512]{1,0:T(8,128)S(1)}, f32[512,512]{1,0:T(8,128)}, u32[]{:S(2)}) copy-start(f32[512,512]{1,0:T(8,128)} %param.12) | copy-start | bytes 3145732
Sparse Core Ops, SparseCore 0:
  9.7 179.7 all-gather.4
  191.4 55.7 all-gather.2
  249.7 107.3 reduce-scatter.1
